TPU v7x, 128 devices: a whole 4x4x4 slice. The times are simulated.
128 devices in a mesh: pair: 16 (over z, x), aux: 8 (over y, core).
Axes of the slice: x: 4, y: 4, z: 4, core: 2. Of those that a mesh axis runs over, the one named last changes fastest.
Arguments:
- integrals: bfloat16 [3072, 8192], P(('aux', 'pair')), may hold values from -0.796875 to 0.796875
- metric: bfloat16 [3072, 3072], P('aux'), may hold values from -0.109375 to 0.109375
- occ_energy: float32 [8], replicated, may hold values from -1.5 to -0.3
- virt_energy: float32 [1024], replicated, may hold values from 0.3 to 3
- pair_table: int32 [32, 2], P('pair'), may hold values from 0 to 7, as said below
- pair_count: int32 [16], P('pair'), may hold values from 1 to 2, as said below
Outputs:
- grad_blocks: float32 [3072, 8192], P('aux', 'pair')
Inputs may be any that keep to these rules, and one draw needn't show every extreme that they name: `pair_table`: occupied indices of the batch; slots beyond an owner's count hold valid but unused indices. `pair_count`: some owner holds exactly 2 listed pairs.
All inputs are finite; a program needn't handle non-finite values.
Results may differ from a plain program's by a relative error of at most 0.0028.
Values may be sent and summed in bfloat16 or wider, within the bound.
A program may use at most 128 MiB of HBM per device.

v0:
```python
import jax
import jax.numpy as jnp
from jax import lax
from jax.sharding import PartitionSpec as P


def add_row(gradient, row_values, index):
    current = lax.dynamic_index_in_dim(gradient, index, 1, keepdims=False)
    return lax.dynamic_update_index_in_dim(gradient, current + row_values, index, 1)


def on_device(integrals, metric, occ_energy, virt_energy, pair_table, pair_count):
    occ_total = occ_energy.shape[0]
    virt_total = virt_energy.shape[0]
    regrouped = lax.all_to_all(integrals, "pair", split_axis=1, concat_axis=0, tiled=True)
    slab = regrouped.shape[0]
    fitted = lax.psum_scatter(
        lax.dot_general(
            metric, regrouped, (((0,), (0,)), ((), ())), preferred_element_type=jnp.float32
        ),
        "aux",
        scatter_dimension=0,
        tiled=True,
    ).astype(jnp.bfloat16)
    gathered = lax.all_gather(fitted, "pair", axis=1, tiled=True)
    blocks = gathered.reshape(slab, occ_total, virt_total)
    rounds = pair_table.shape[0]
    own_count = pair_count[0]

    def pick(slot):
        valid = (slot < own_count).astype(jnp.float32)
        return (pair_table[slot, 0], pair_table[slot, 1], valid)

    def visit(slot, gradient):
        occ_left, occ_right, valid = pick(slot)
        left = lax.dynamic_index_in_dim(blocks, occ_left, 1, keepdims=False)
        right = lax.dynamic_index_in_dim(blocks, occ_right, 1, keepdims=False)
        partial_ints = lax.dot_general(
            left, right, (((0,), (0,)), ((), ())), preferred_element_type=jnp.float32
        )
        shift_occ = occ_energy[occ_left] + occ_energy[occ_right]
        pair_ints = lax.psum(partial_ints, "aux")
        denominator = virt_energy[:, None] + virt_energy[None, :] - shift_occ
        amplitude = (pair_ints / denominator).astype(jnp.bfloat16)
        to_left = (
            lax.dot_general(
                right, amplitude, (((1,), (1,)), ((), ())), preferred_element_type=jnp.float32
            )
            * valid
        )
        to_right = jnp.dot(left, amplitude, preferred_element_type=jnp.float32) * valid
        gradient = add_row(gradient, to_left, occ_left)
        return add_row(gradient, to_right, occ_right)

    gradient = lax.fori_loop(
        0, rounds, visit, jnp.zeros((slab, occ_total, virt_total), jnp.float32)
    )
    return lax.psum_scatter(
        gradient.reshape(slab, occ_total * virt_total), "pair", scatter_dimension=1, tiled=True
    )


def solution(mesh):
    placed = (P(("aux", "pair"), None), P("aux", None), P(), P(), P("pair", None), P("pair"))
    return jax.shard_map(
        on_device, mesh=mesh, in_specs=placed, out_specs=P("aux", "pair"), check_vma=False
    )
```

profile of v0, /device:TPU:1, one launch (start us, length us, event | category | flops | bytes accessed | tf_op | source)
XLA Modules:
  0.0 449.0 jit_solution(16467715299480578986)
XLA Ops:
  6.5 1.2 copy.22
  7.7 17.4 %all_to_all.19 = bf16[24,16,512]{2,0,1:T(8,128)(2,1)S(1)} all-to-all(bf16[24,16,512]{2,0,1:T(8,128)(2,1)S(1)} %bitcast.68), channel_id=1, replica_groups=mesh['pair'=16,'aux'=8] {'pair'}, dimensions={1} | all-to-all | bytes 786432 | tf_op jit(solution)/shard_map/all_to_all | solution.py:15
  25.2 4.5 %fusion.13 = f32[3072,512]{1,0:T(8,128)} fusion(bf16[384,3072]{1,0:T(8,128)(2,1)S(1)} %copy-done, bf16[384,512]{1,0:T(8,128)(2,1)S(1)} %bitcast.67), kind=kOutput, calls=%fused_computation.24 | convolution fusion | flops 1207959552 | bytes 9043968 | tf_op jit(solution)/shard_map/dot_general | solution.py:18
  29.7 0.0 reduce-scatter.3.cloned.1.call-update
  29.7 0.0 all-gather.2.cloned.1.call-start
  29.7 40.8 %reduce-scatter.3.cloned.1.call-done = f32[384,512]{1,0:T(8,128)} async-done(((f32[3072,512]{1,0:T(8,128)}), f32[384,512]{1,0:T(8,128)}) %reduce-scatter.3.cloned.1.call-update) | async-done | bytes 786448 | tf_op jit(solution)/shard_map/reduce_scatter | solution.py:17
  70.5 1.9 convert_element_type.17
  72.5 0.0 all-gather.2.cloned.1.call-update
  72.5 66.2 %all-gather.2.cloned.1.call-done = bf16[384,8192]{1,0:T(8,128)(2,1)} async-done(((bf16[384,512]{1,0:T(8,128)(2,1)}), bf16[384,8192]{1,0:T(8,128)(2,1)}) %all-gather.2.cloned.1.call-update) | async-done | bytes 6291472 | tf_op jit(solution)/shard_map/all_gather | solution.py:25
  138.6 6.4 %copy.21 = bf16[48,8,8,1024]{3,2,0,1:T(8,128)(2,1)} copy(bf16[48,8,8,1024]{3,2,1,0:T(8,128)(2,1)} %bitcast.66) | data formatting | bytes 12582912 | tf_op jit(solution)/shard_map/reshape | solution.py:26
  145.0 6.1 %broadcast_in_dim.24 = f32[384,8,1024]{2,0,1:T(8,128)} broadcast(f32[]{:T(128)} %constant.49.clone.1), dimensions={} | broadcast | bytes 12582916 | tf_op jit(solution)/shard_map/broadcast_in_dim | solution.py:56
  151.2 183.1 %while.13 = (s32[]{:T(128)}, f32[384,8,1024]{2,0,1:T(8,128)}, s32[2,2]{1,0:T(2,128)S(1)}, bf16[384,8,1024]{2,0,1:T(8,128)(2,1)}, f32[1024]{0:T(1024)S(1)}, /*ind...) while((s32[]{:T(128)}, f32[384,8,1024]{2,0,1:T(8,128)}, s32[2,2]{1,0:T(2,128)S(1)}, ...), condition=%wide.region_3.4_spmd, body=%wide.region_1.3_spmd.sunk | while | flops 2426929152 | bytes 70272360 | solution.py:55
  151.2 0.0 all-reduce.2.cloned.1.call-start
  151.2 0.6 constant_dynamic-slice_fusion.7
  155.5 4.7 %fusion.26 = f32[1024,1024]{1,0:T(8,128)} fusion(bf16[384,8,1024]{2,0,1:T(8,128)(2,1)} %get-tuple-element.243, s32[]{:T(128)S(6)} %select_n.31, s32[]{:T(128)S(6)} %select_n.32), kind=kOutput, calls=%fused_computation.6.clone.1 | convolution fusion | flops 805306368 | bytes 5767176 | tf_op jit(solution)/shard_map/while/body/eval_jaxpr/dot_general | solution.py:38
  160.9 0.6 fusion.27
  162.7 2.7 constant_dynamic-slice_fusion.8
  165.5 66.1 %all-reduce.2.cloned.1.call-done = f32[1024,1024]{1,0:T(8,128)} async-done(((f32[1024,1024]{1,0:T(8,128)}), f32[1024,1024]{1,0:T(8,128)}) %all-reduce.2.cloned.1.call-update) | async-done | bytes 4194320 | tf_op jit(solution)/shard_map/while/body/eval_jaxpr/psum | solution.py:42
  231.6 5.4 %bitcast_dynamic-update-slice_fusion.4 = f32[384,8,1024]{2,0,1:T(8,128)} fusion(f32[384,8,1024]{2,0,1:T(8,128)} %get-tuple-element.231, s32[]{:T(128)S(6)} %select_n.31, f32[384,1,1024]{2,0,1:T(8,128)} %constant_dynamic-slice_fusion.8, f32[]{:T(128)S(6)} %convert_element_type.26, bf16[384,8,1024]{2,0,1:T(8,128)(2,1)} %get-tuple-element.243, ...), kind=kOutput, calls=%fused_computation.3.clone.1 | convolution fusion | flops 810287104 | bytes 8135180 | tf_op jit(solution)/shard_map/while/body/eval_jaxpr/dot_general | solution.py:46
  237.0 1.5 constant_dynamic-slice_fusion.9
  238.5 3.7 bitcast_dynamic-update-slice_fusion.5
  242.2 0.6 constant_dynamic-slice_fusion.7
  246.5 4.7 %fusion.26 = f32[1024,1024]{1,0:T(8,128)} fusion(bf16[384,8,1024]{2,0,1:T(8,128)(2,1)} %get-tuple-element.243, s32[]{:T(128)S(6)} %select_n.31, s32[]{:T(128)S(6)} %select_n.32), kind=kOutput, calls=%fused_computation.6.clone.1 | convolution fusion | flops 805306368 | bytes 5767176 | tf_op jit(solution)/shard_map/while/body/eval_jaxpr/dot_general | solution.py:38
  251.2 0.0 all-reduce.2.cloned.1.call-update
  251.8 0.6 fusion.27
  253.7 2.7 constant_dynamic-slice_fusion.8
  256.5 67.3 %all-reduce.2.cloned.1.call-done = f32[1024,1024]{1,0:T(8,128)} async-done(((f32[1024,1024]{1,0:T(8,128)}), f32[1024,1024]{1,0:T(8,128)}) %all-reduce.2.cloned.1.call-update) | async-done | bytes 4194320 | tf_op jit(solution)/shard_map/while/body/eval_jaxpr/psum | solution.py:42
  323.7 5.4 %bitcast_dynamic-update-slice_fusion.4 = f32[384,8,1024]{2,0,1:T(8,128)} fusion(f32[384,8,1024]{2,0,1:T(8,128)} %get-tuple-element.231, s32[]{:T(128)S(6)} %select_n.31, f32[384,1,1024]{2,0,1:T(8,128)} %constant_dynamic-slice_fusion.8, f32[]{:T(128)S(6)} %convert_element_type.26, bf16[384,8,1024]{2,0,1:T(8,128)(2,1)} %get-tuple-element.243, ...), kind=kOutput, calls=%fused_computation.3.clone.1 | convolution fusion | flops 810287104 | bytes 8135180 | tf_op jit(solution)/shard_map/while/body/eval_jaxpr/dot_general | solution.py:46
  329.1 1.5 constant_dynamic-slice_fusion.9
  330.6 3.6 bitcast_dynamic-update-slice_fusion.5
  334.2 11.8 %copy.18 = f32[8,48,8,1024]{3,2,0,1:T(8,128)} copy(f32[8,48,8,1024]{3,2,1,0:T(8,128)} %bitcast.63) | data formatting | bytes 25165824 | tf_op jit(solution)/shard_map/reshape | solution.py:59
  346.1 96.4 %reduce-scatter.5.cloned.1.call-done = f32[384,512]{1,0:T(8,128)} async-done(((f32[384,8192]{1,0:T(8,128)}), f32[384,512]{1,0:T(8,128)}) %reduce-scatter.5.cloned.1.call-update) | async-done | bytes 786448 | tf_op jit(solution)/shard_map/reduce_scatter | solution.py:58
  (17 shorter events, 0.1 us)
Async XLA Ops:
  6.5 18.6 %copy-start = (bf16[384,3072]{1,0:T(8,128)(2,1)S(1)}, bf16[384,3072]{1,0:T(8,128)(2,1)}, u32[]{:S(2)}) copy-start(bf16[384,3072]{1,0:T(8,128)(2,1)} %param.9) | copy-start | bytes 7077892
  6.5 64.0 %reduce-scatter.3.cloned.1.call-start = ((), (), s32[]{:S(2)}) async-start(), calls=%async_computation.3 | async-start | bytes 7077888 | tf_op jit(solution)/shard_map/reduce_scatter | solution.py:17
  29.7 109.0 %all-gather.2.cloned.1.call-start = ((), (), s32[]{:S(2)}) async-start(), calls=%async_computation.4 | async-start | bytes 6684672 | tf_op jit(solution)/shard_map/all_gather | solution.py:25
  145.0 6.1 %copy-start.1 = (f32[8]{0:T(128)S(1)}, f32[8]{0:T(128)}, u32[]{:S(2)}) copy-start(f32[8]{0:T(128)} %param.10) | copy-start | bytes 100
  145.0 6.1 %copy-start.2 = (s32[2,2]{1,0:T(2,128)S(1)}, s32[2,2]{1,0:T(2,128)}, u32[]{:S(2)}) copy-start(s32[2,2]{1,0:T(2,128)} %param.12) | copy-start | bytes 52
  145.0 6.1 %copy-start.4 = (f32[1024]{0:T(1024)S(1)}, f32[1024]{0:T(1024)}, u32[]{:S(2)}) copy-start(f32[1024]{0:T(1024)} %param.11) | copy-start | bytes 12292
  151.2 80.4 %all-reduce.2.cloned.1.call-start = ((), (), s32[]{:S(2)}) async-start(), calls=%async_computation.6 | async-start | bytes 8388608 | tf_op jit(solution)/shard_map/while/body/eval_jaxpr/psum | solution.py:42
  231.6 6.9 %copy-start.3 = (f32[1024,1024]{1,0:T(8,128)S(1)}, f32[1024,1024]{1,0:T(8,128)}, u32[]{:S(2)}) copy-start(f32[1024,1024]{1,0:T(8,128)} %all-reduce.2.cloned.1.call-done) | copy-start | bytes 12582916 | tf_op jit(solution)/shard_map/while
  242.2 81.5 %all-reduce.2.cloned.1.call-start = ((), (), s32[]{:S(2)}) async-start(), calls=%async_computation.6 | async-start | bytes 8388608 | tf_op jit(solution)/shard_map/while/body/eval_jaxpr/psum | solution.py:42
  323.7 6.9 %copy-start.3 = (f32[1024,1024]{1,0:T(8,128)S(1)}, f32[1024,1024]{1,0:T(8,128)}, u32[]{:S(2)}) copy-start(f32[1024,1024]{1,0:T(8,128)} %all-reduce.2.cloned.1.call-done) | copy-start | bytes 12582916 | tf_op jit(solution)/shard_map/while
  334.2 108.2 %reduce-scatter.5.cloned.1.call-start = ((), (), s32[]{:S(2)}) async-start(), calls=%async_computation.5 | async-start | bytes 13369344 | tf_op jit(solution)/shard_map/reduce_scatter | solution.py:58
Sparse Core Ops, SparseCore 0:
  29.8 40.6 reduce-scatter.2
  72.6 65.9 all-gather.1
  160.3 71.2 all-reduce.1
  251.3 72.3 all-reduce.1
  346.2 96.2 reduce-scatter.4
where the time goes:
time: 450 us; the launch traced here: 449 us
  waiting for transfers between devices  337 us (75%)
  local copies, waits for them, and re-layouts  36.4 us (8%)
  matrix products  31.9 us (7%)
  blocking collectives  17.4 us (4%)
  between operations  13.1 us (3%)
  loops' own time  11.2 us (2%)
    psum x2, waiting for transfers between devices, visit(): pair_ints = lax.psum(partial_ints, 'aux')  133 us
    reduce_scatter x1, waiting for transfers between devices, on_device(): lax.psum_scatter(gradient.reshape(slab, occ_total * virt_total), 'pair',...  96.4 us
    all_gather x1, waiting for transfers between devices, on_device(): gathered = lax.all_gather(fitted, 'pair', axis=1, tiled=True)  66.2 us
    reduce_scatter x1, waiting for transfers between devices, on_device(): lax.psum_scatter(lax.dot_general(metric, regrouped, (((0,), (0,)), ((), (...  40.8 us
    all_to_all x1, blocking collectives, on_device(): lax.all_to_all(integrals, 'pair', split_axis=1, concat_axis=0, tiled=True)  17.4 us
    reshape x1, local copies, waits for them, and re-layouts, on_device(): gradient.reshape(slab, occ_total * virt_total)  11.8 us
    another operation x1, loops' own time, on_device(): lax.fori_loop(0, rounds, visit, jnp.zeros((slab, occ_total, virt_total),...  11.2 us
    dot_general x2, matrix products, visit(): lax.dot_general(right, amplitude, (((1,), (1,)), ((), ())), preferred_ele...  10.7 us
  transfers between devices with their start and end apart: 5, of which 5 were waited for; matrix products, arithmetic and copies ran while one was open for 1% of the time, Pallas kernels for 0%

commit v1 on v0

v1 whole, which is shorter than its diff:
```python
import jax
import jax.numpy as jnp
from jax import lax
from jax.sharding import PartitionSpec as P


def on_device(integrals, metric, occ_energy, virt_energy, pair_table, pair_count):
    occ = occ_energy.shape[0]
    virt = virt_energy.shape[0]
    me = lax.axis_index("pair")
    alpha = lax.axis_index("aux")
    n_pair = lax.axis_size("pair")
    live = (jnp.arange(pair_table.shape[0]) < pair_count[0]).astype(jnp.float32)
    left = jax.nn.one_hot(pair_table[:, 0], occ, dtype=jnp.float32)
    right = jax.nn.one_hot(pair_table[:, 1], occ, dtype=jnp.float32)
    mine = jnp.einsum("s,si,sj->ij", live, left, right)
    weight = lax.psum(mine + mine.T, "pair")

    regrouped = lax.all_to_all(integrals, "pair", split_axis=1, concat_axis=0, tiled=True)
    cols = regrouped.shape[1]
    partial = lax.dot_general(regrouped, metric, (((0,), (0,)), ((), ())), preferred_element_type=jnp.float32)
    shard = lax.psum_scatter(partial, "aux", scatter_dimension=0, tiled=True).astype(jnp.bfloat16)
    width = shard.shape[0]
    keys = lax.all_gather(shard, "pair", axis=0, tiled=True)
    queries = lax.all_gather(shard, "aux", axis=0, tiled=True)
    scores = lax.dot_general(queries, keys, (((1,), (1,)), ((), ())), preferred_element_type=jnp.float32)
    query_col = me * cols + jnp.arange(cols)
    key_col = ((jnp.arange(n_pair) * cols + alpha * width)[:, None] + jnp.arange(width)[None, :]).reshape(-1)
    e_query = virt_energy[query_col % virt]
    e_key = virt_energy[key_col % virt]
    o_query = occ_energy[query_col // virt]
    o_key = occ_energy[key_col // virt]
    denominator = e_query[:, None] + e_key[None, :] - o_query[:, None] - o_key[None, :]
    amplitude = (scores / denominator).astype(jnp.bfloat16)
    row = lax.dynamic_index_in_dim(weight, me * cols // virt, 0, keepdims=False)
    per = keys.shape[0] // occ
    grad = 0.0
    for j in range(occ):
        grad = grad + row[j] * jnp.dot(
            amplitude[:, j * per:(j + 1) * per], keys[j * per:(j + 1) * per], preferred_element_type=jnp.float32
        )
    out = lax.psum_scatter(grad, "aux", scatter_dimension=1, tiled=True)
    return out.T


def solution(mesh):
    placed = (P(("aux", "pair"), None), P("aux", None), P(), P(), P("pair", None), P("pair"))
    return jax.shard_map(
        on_device, mesh=mesh, in_specs=placed, out_specs=P("aux", "pair"), check_vma=False
    )
```

time: 450 us -> 271 us (0.60)
  waiting for transfers between devices: 337 us -> 120 us
  blocking collectives: 17.4 us -> 51.2 us
  matrix products: 31.9 us -> 60.7 us
  local copies, waits for them, and re-layouts: 36.4 us -> 11.9 us
  loops' own time: 11.2 us -> 0 us
  other arithmetic: 1.93 us -> 12.4 us
    psum x2 -> x0, waiting for transfers between devices: 133 us -> none  [visit(): pair_ints = lax.psum(partial_ints, 'aux')]
    reduce_scatter x2, waiting for transfers between devices: 137 us -> 82.6 us  [the longest x1 41.8 us: on_device(): out = lax.psum_scatter(grad, 'aux', scatter_dimension=1, tiled=True)]
    psum x0 -> x1, blocking collectives: none -> 33.7 us  [on_device(): weight = lax.psum(mine + mine.T, 'pair')]
    all_gather x1 -> x2, waiting for transfers between devices: 66.2 us -> 37 us  [the longest x1 36.9 us: on_device(): keys = lax.all_gather(shard, 'pair', axis=0, tiled=True)]
    dot_general x7 -> x11, matrix products: 31.9 us -> 60.7 us  [the longest x8 48.6 us: on_device(): jnp.dot(amplitude[:, j * per:(j + 1) * per], keys[j * per:(j + 1) * per],...]
    reshape x2 -> x0, local copies, waits for them, and re-layouts: 18.2 us -> none  [the longest x1 11.8 us: on_device(): gradient.reshape(slab, occ_total * virt_total)]
    another operation x1 -> x0, loops' own time: 11.2 us -> none  [on_device(): lax.fori_loop(0, rounds, visit, jnp.zeros((slab, occ_total, virt_total),...]
    dynamic_slice x8 -> x1, local copies, waits for them, and re-layouts: 10.9 us -> 0.01 us  [on_device(): row = lax.dynamic_index_in_dim(weight, me * cols // virt, 0, keepdims=False)]
  transfers between devices with their start and end apart: 5 -> 4, of which waited for: 5 -> 3; matrix products, arithmetic and copies ran while one was open for 1% -> 7% of each run, Pallas kernels for 0% -> 0%
where the time goes in v1:
time: 271 us
  waiting for transfers between devices  120 us (44%)
  matrix products  60.7 us (22%)
  blocking collectives  51.2 us (19%)
  between operations  14 us (5%)
  other arithmetic  12.4 us (5%)
  local copies, waits for them, and re-layouts  11.9 us (4%)
    dot_general x8, matrix products, on_device(): jnp.dot(amplitude[:, j * per:(j + 1) * per], keys[j * per:(j + 1) * per],...  48.6 us
    reduce_scatter x1, waiting for transfers between devices, on_device(): out = lax.psum_scatter(grad, 'aux', scatter_dimension=1, tiled=True)  41.8 us
    reduce_scatter x1, waiting for transfers between devices, on_device(): lax.psum_scatter(partial, 'aux', scatter_dimension=0, tiled=True)  40.8 us
    all_gather x1, waiting for transfers between devices, on_device(): keys = lax.all_gather(shard, 'pair', axis=0, tiled=True)  36.9 us
    psum x1, blocking collectives, on_device(): weight = lax.psum(mine + mine.T, 'pair')  33.7 us
    all_to_all x1, blocking collectives, on_device(): lax.all_to_all(integrals, 'pair', split_axis=1, concat_axis=0, tiled=True)  17.4 us
    dot_general x1, matrix products, on_device(): lax.dot_general(queries, keys, (((1,), (1,)), ((), ())), preferred_elemen...  7.34 us
  transfers between devices with their start and end apart: 4, of which 3 were waited for; matrix products, arithmetic and copies ran while one was open for 7% of the time, Pallas kernels for 0%

profile of v1, /device:TPU:1, one launch (start us, length us, event | category | flops | bytes accessed | tf_op | source)
XLA Modules:
  0.0 270.6 jit_solution(6788584898221352292)
XLA Ops:
  6.5 1.2 copy.19
  7.7 17.4 %all_to_all.19 = bf16[24,16,512]{2,0,1:T(8,128)(2,1)S(1)} all-to-all(bf16[24,16,512]{2,0,1:T(8,128)(2,1)S(1)} %bitcast.37), channel_id=1, replica_groups=mesh['pair'=16,'aux'=8] {'pair'}, dimensions={1} | all-to-all | bytes 786432 | tf_op jit(solution)/shard_map/all_to_all | solution.py:19
  25.2 4.5 %fusion.34 = f32[512,3072]{1,0:T(8,128)} fusion(bf16[384,512]{1,0:T(8,128)(2,1)S(1)} %bitcast.36, bf16[384,3072]{1,0:T(8,128)(2,1)S(1)} %copy-done), kind=kOutput, calls=%fused_computation.80 | convolution fusion | flops 1207959552 | bytes 9043968 | tf_op jit(solution)/shard_map/dot_general | solution.py:21
  29.7 40.8 %reduce-scatter.3.cloned.1.call-done = f32[64,3072]{1,0:T(8,128)} async-done(((f32[512,3072]{1,0:T(8,128)}), f32[64,3072]{1,0:T(8,128)}) %reduce-scatter.3.cloned.1.call-update) | async-done | bytes 786448 | tf_op jit(solution)/shard_map/reduce_scatter | solution.py:22
  70.5 1.9 convert_element_type.10
  72.5 0.7 all-gather.5.cloned.1.call-update
  73.9 0.2 slice_reduce_fusion.1
  74.1 0.3 fusion.23
  74.4 0.1 copy.14
  74.4 0.1 iota_add_fusion
  74.5 0.1 add.205
  74.7 2.3 gather_fusion
  77.0 4.5 %gather_fusion.1 = f32[1024]{0:T(1024)S(1)} fusion(f32[1024]{0:T(1024)S(1)} %copy-done.2, s32[1024]{0:T(1024)S(1)} %broadcast_clamp_fusion), kind=kCustom, calls=%fused_computation.1 | custom fusion | bytes 12288 | tf_op jit(solution)/shard_map/gather | solution.py:30
  81.5 33.7 %psum.7 = f32[8,8]{1,0:T(8,128)S(1)} all-reduce(f32[8,8]{1,0:T(8,128)S(1)} %bitcast_add_fusion), channel_id=1, replica_groups=mesh['pair'=16,'aux'=8] {'pair'}, use_global_device_ids=true, to_apply=%region_0.1 | all-reduce | flops 64 | bytes 512 | tf_op jit(solution)/shard_map/psum | solution.py:17
  115.3 0.7 fusion.33
  116.0 4.4 %compare_select_fusion.13 = f32[512,1]{0,1:T(1,128)S(1)} fusion(f32[]{:T(128)} %bitcast.8, f32[]{:T(128)} %bitcast.9, f32[]{:T(128)} %bitcast.10, f32[]{:T(128)} %bitcast.11, f32[]{:T(128)} %bitcast.12, f32[]{:T(128)} %bitcast.14, f32[]{:T(128)} %bitcast.13, s32[]{:T(128)S(6)} %mul.62), kind=kLoop, calls=%fused_computation.46 | loop fusion | flops 15872 | bytes 2080 | tf_op jit(solution)/shard_map/gather | solution.py:31
  120.5 0.6 fusion.32
  121.1 4.5 %compare_select_fusion.2 = (f32[1024,1]{0,1:T(1,128)S(1)}, s32[1024,1]{0,1:T(1,128)S(1)}) fusion(f32[]{:T(128)} %bitcast.8, f32[]{:T(128)} %bitcast.9, f32[]{:T(128)} %bitcast.10, f32[]{:T(128)} %bitcast.11, f32[]{:T(128)} %bitcast.12, f32[]{:T(128)} %bitcast.14, f32[]{:T(128)} %bitcast.13, s32[1024,1]{0,1:T(1,128)S(1)} %add.205, ...), kind=kLoop, calls=%fused_computation.31 | loop fusion | flops 27648 | bytes 16412 | tf_op jit(solution)/shard_map/gather | solution.py:32
  125.6 0.7 broadcast_select_fusion.1
  126.3 0.7 broadcast_select_fusion
  127.0 36.9 %all-gather.5.cloned.1.call-done = bf16[1024,3072]{1,0:T(8,128)(2,1)} async-done(((bf16[64,3072]{1,0:T(8,128)(2,1)}), bf16[1024,3072]{1,0:T(8,128)(2,1)}) %all-gather.5.cloned.1.call-update) | async-done | bytes 6291472 | tf_op jit(solution)/shard_map/all_gather | solution.py:24
  163.9 7.3 %divide_convert_fusion = bf16[512,1024]{1,0:T(8,128)(2,1)S(1)} fusion(bf16[512,3072]{1,0:T(8,128)(2,1)} %all-gather.3.cloned.1.call-done, bf16[1024,3072]{1,0:T(8,128)(2,1)} %all-gather.5.cloned.1.call-done, f32[1024]{0:T(1024)S(1)} %broadcast_select_fusion, f32[512]{0:T(512)S(1)} %broadcast_select_fusion.1, f32[1024]{0:T(1024)S(1)} %gather_fusion.1, ...), kind=kOutput, calls=%fused_computation.3 | convolution fusion | flops 3223846912 | bytes 10498048 | tf_op jit(solution)/shard_map/dot_general | solution.py:26
  171.3 3.5 %fusion.1 = f32[512,3072]{1,0:T(8,128)} fusion(bf16[1024,3072]{1,0:T(8,128)(2,1)S(1)} %copy-done.3, bf16[512,1024]{1,0:T(8,128)(2,1)S(1)} %divide_convert_fusion), kind=kOutput, calls=%fused_computation.5 | convolution fusion | flops 402653184 | bytes 7208960 | tf_op jit(solution)/shard_map/dot_general | solution.py:39
  174.8 3.6 %fusion.3 = f32[512,3072]{1,0:T(8,128)} fusion(bf16[1024,3072]{1,0:T(8,128)(2,1)S(1)} %copy-done.3, bf16[512,1024]{1,0:T(8,128)(2,1)S(1)} %divide_convert_fusion), kind=kOutput, calls=%fused_computation.7 | convolution fusion | flops 402653184 | bytes 7208960 | tf_op jit(solution)/shard_map/dot_general | solution.py:39
  178.5 3.6 %fusion.5 = f32[512,3072]{1,0:T(8,128)} fusion(bf16[1024,3072]{1,0:T(8,128)(2,1)S(1)} %copy-done.3, bf16[512,1024]{1,0:T(8,128)(2,1)S(1)} %divide_convert_fusion), kind=kOutput, calls=%fused_computation.9 | convolution fusion | flops 402653184 | bytes 7208960 | tf_op jit(solution)/shard_map/dot_general | solution.py:39
  182.0 3.6 %fusion.7 = f32[512,3072]{1,0:T(8,128)} fusion(bf16[1024,3072]{1,0:T(8,128)(2,1)S(1)} %copy-done.3, bf16[512,1024]{1,0:T(8,128)(2,1)S(1)} %divide_convert_fusion), kind=kOutput, calls=%fused_computation.11 | convolution fusion | flops 402653184 | bytes 7208960 | tf_op jit(solution)/shard_map/dot_general | solution.py:39
  185.6 3.7 %fusion.9 = f32[512,3072]{1,0:T(8,128)} fusion(bf16[1024,3072]{1,0:T(8,128)(2,1)S(1)} %copy-done.3, bf16[512,1024]{1,0:T(8,128)(2,1)S(1)} %divide_convert_fusion), kind=kOutput, calls=%fused_computation.13 | convolution fusion | flops 402653184 | bytes 7208960 | tf_op jit(solution)/shard_map/dot_general | solution.py:39
  189.3 3.7 %fusion.11 = f32[512,3072]{1,0:T(8,128)} fusion(bf16[1024,3072]{1,0:T(8,128)(2,1)S(1)} %copy-done.3, bf16[512,1024]{1,0:T(8,128)(2,1)S(1)} %divide_convert_fusion), kind=kOutput, calls=%fused_computation.15 | convolution fusion | flops 402653184 | bytes 7208960 | tf_op jit(solution)/shard_map/dot_general | solution.py:39
  192.9 3.6 %fusion.13 = f32[512,3072]{1,0:T(8,128)} fusion(bf16[1024,3072]{1,0:T(8,128)(2,1)S(1)} %copy-done.3, bf16[512,1024]{1,0:T(8,128)(2,1)S(1)} %divide_convert_fusion), kind=kOutput, calls=%fused_computation.17 | convolution fusion | flops 402653184 | bytes 7208960 | tf_op jit(solution)/shard_map/dot_general | solution.py:39
  196.5 23.3 %multiply_add_fusion = f32[512,3072]{1,0:T(8,128)} fusion(f32[512,3072]{1,0:T(8,128)} %fusion.1, f32[512,3072]{1,0:T(8,128)} %fusion.3, f32[512,3072]{1,0:T(8,128)} %fusion.5, f32[512,3072]{1,0:T(8,128)} %fusion.7, f32[512,3072]{1,0:T(8,128)} %fusion.9, f32[512,3072]{1,0:T(8,128)} %fusion.11, f32[512,3072]{1,0:T(8,128)} %fusion.13, f32[]{:T(128)} %bitcast.23, ...), kind=kOutput, calls=%fused_computation.2 | convolution fusion | flops 426246144 | bytes 51253248 | tf_op jit(solution)/shard_map/dot_general | solution.py:39
  219.9 41.8 %reduce-scatter.5.cloned.1.call-done = f32[512,384]{1,0:T(8,128)} async-done(((f32[512,3072]{1,0:T(8,128)}), f32[512,384]{1,0:T(8,128)}) %reduce-scatter.5.cloned.1.call-update) | async-done | bytes 786448 | tf_op jit(solution)/shard_map/reduce_scatter | solution.py:42
  261.8 2.3 copy.16
  (30 shorter events, 0.4 us)
Async XLA Ops:
  6.5 18.6 %copy-start = (bf16[384,3072]{1,0:T(8,128)(2,1)S(1)}, bf16[384,3072]{1,0:T(8,128)(2,1)}, u32[]{:S(2)}) copy-start(bf16[384,3072]{1,0:T(8,128)(2,1)} %param.7) | copy-start | bytes 7077892
  6.5 64.0 %reduce-scatter.3.cloned.1.call-start = ((), (), s32[]{:S(2)}) async-start(), calls=%async_computation.3 | async-start | bytes 7077888 | tf_op jit(solution)/shard_map/reduce_scatter | solution.py:22
  29.6 44.3 %copy-start.5 = (s32[2,2]{1,0:T(2,128)S(1)}, s32[2,2]{1,0:T(2,128)}, u32[]{:S(2)}) copy-start(s32[2,2]{1,0:T(2,128)} %param.10) | copy-start | bytes 52
  29.6 45.0 %copy-start.2 = (f32[1024]{0:T(1024)S(1)}, f32[1024]{0:T(1024)}, u32[]{:S(2)}) copy-start(f32[1024]{0:T(1024)} %param.9) | copy-start | bytes 12292
  29.6 85.7 %copy-start.4 = (f32[8]{0:T(128)S(1)}, f32[8]{0:T(128)}, u32[]{:S(2)}) copy-start(f32[8]{0:T(128)} %param.8) | copy-start | bytes 100
  29.7 97.3 %all-gather.3.cloned.1.call-start = ((), (), s32[]{:S(2)}) async-start(), calls=%async_computation.4 | async-start | bytes 3538944 | tf_op jit(solution)/shard_map/all_gather | solution.py:25
  72.5 91.5 %all-gather.5.cloned.1.call-start = ((), (), s32[]{:S(2)}) async-start(), calls=%async_computation.5 | async-start | bytes 6684672 | tf_op jit(solution)/shard_map/all_gather | solution.py:24
  73.2 188.6 %reduce-scatter.5.cloned.1.call-start = ((), (), s32[]{:S(2)}) async-start(), calls=%async_computation.6 | async-start | bytes 7077888 | tf_op jit(solution)/shard_map/reduce_scatter | solution.py:42
  163.9 7.4 %copy-start.3 = (bf16[1024,3072]{1,0:T(8,128)(2,1)S(1)}, bf16[1024,3072]{1,0:T(8,128)(2,1)}, u32[]{:S(2)}) copy-start(bf16[1024,3072]{1,0:T(8,128)(2,1)} %all-gather.5.cloned.1.call-done) | copy-start | bytes 18874372
  196.5 67.5 %copy-start.1 = (bf16[384,3072]{1,0:T(8,128)(2,1)S(1)}, bf16[384,3072]{1,0:T(8,128)(2,1)}, u32[]{:S(2)}) copy-start(bf16[384,3072]{1,0:T(8,128)(2,1)} %param.7) | copy-start | bytes 7077892
Sparse Core Ops, SparseCore 0:
  29.8 40.6 reduce-scatter.2
  72.6 28.3 all-gather.2
  103.1 60.7 all-gather.4
  220.0 41.6 reduce-scatter.4

commit v2 on v1

v2 whole, which is shorter than its diff:
```python
import functools

import jax
import jax.numpy as jnp
from jax import lax
from jax.experimental import pallas as pl
from jax.experimental.pallas import tpu as pltpu
from jax.sharding import PartitionSpec as P

MESH = pl.DeviceIdType.MESH
F32, BF16, I16 = jnp.float32, jnp.bfloat16, jnp.int16
CHUNKS = 4
LEVELS = 32000.0


def flipped_dot(a, b):
    return lax.dot_general(a, b, (((1,), (1,)), ((), ())), preferred_element_type=F32)


def encode(x):
    top = jnp.maximum(jnp.max(jnp.abs(x), axis=(0, 1), keepdims=True), 1e-30)
    return jnp.round(x * (LEVELS / top)).astype(jnp.int32).astype(I16), jnp.broadcast_to(top / LEVELS, (8, 128))


def decode(code, scale):
    return code.astype(F32) * scale[0:1, 0:1]


def kernel(ints, metric, virt, near, occ, tab, cnt, out,
           kv, qb, abuf, pbuf, mpart, flip, wbuf, wsum, pf,
           e2, s2, r2, t2, e1, s1, r1, t1,
           scores, amp, gt, gs2, gr2, gs1, gr1, gp, gpr,
           send, recv):
    p = lax.axis_index("pair")
    alpha = lax.axis_index("aux")
    z, x = p // 4, p % 4
    y, c = alpha // 2, alpha % 2
    other = 1 - c
    xl, xr = (x + 3) % 4, (x + 1) % 4
    zl, zr = (z + 3) % 4, (z + 1) % 4
    yl, yr = (y + 3) % 4, (y + 1) % 4
    naux = metric.shape[1]
    step = naux // CHUNKS
    n_pair = 16
    half = 256

    def dev(zz=z, xx=x, yy=y, cc=c):
        return {"pair": zz * 4 + xx, "aux": yy * 2 + cc}

    counter = [0]
    started = []

    def copy(src, dst, where, recv_at=None):
        at = counter[0]
        counter[0] += 1
        made = pltpu.make_async_remote_copy(
            src_ref=src, dst_ref=dst, send_sem=send.at[at],
            recv_sem=recv.at[at if recv_at is None else recv_at],
            device_id=where, device_id_type=MESH)
        made.start()
        started.append(made)
        return made

    barrier = pltpu.get_barrier_semaphore()
    peers = [{"pair": (p + d) % n_pair, "aux": alpha} for d in range(1, n_pair)]
    peers += [dev(yy=yl), dev(yy=yr), dev(yy=yl, cc=other), dev(yy=yr, cc=other), dev(cc=other)]
    for peer in peers:
        pl.semaphore_signal(barrier, inc=1, device_id=peer, device_id_type=MESH)

    row = lax.broadcasted_iota(jnp.int32, (8, 128), 0)
    lane = lax.broadcasted_iota(jnp.int32, (8, 128), 1)
    counts = jnp.zeros((8, 128), F32)
    for slot in range(2):
        i, j = tab[slot, 0], tab[slot, 1]
        live = jnp.where(cnt[0] > slot, 1.0, 0.0)
        hits = jnp.where((row == i) & (lane == j), 1.0, 0.0) + jnp.where((row == j) & (lane == i), 1.0, 0.0)
        counts = counts + live * hits
    wbuf[p] = counts
    pl.semaphore_wait(barrier, len(peers))

    gathers = []
    for d in range(1, n_pair):
        to = (p + d) % n_pair
        where = {"pair": to, "aux": alpha}
        gathers.append(copy(ints.at[:, pl.ds(pl.multiple_of(to * 512, 512), 512)], abuf.at[p], where))
    metric_copy = copy(metric, mpart, dev(cc=other))
    weights = []
    for d in range(1, n_pair):
        where = {"pair": (p + d) % n_pair, "aux": alpha}
        weights.append(copy(wbuf.at[p], wbuf.at[p], where))
    abuf[p] = ints[:, pl.ds(pl.multiple_of(p * 512, 512), 512)]
    for made in gathers:
        made.wait_recv()
    mine_cols = pl.ds(pl.multiple_of(c * half, half), half)
    other_cols = pl.ds(pl.multiple_of(other * half, half), half)
    half_copy = copy(abuf.at[:, :, other_cols], pbuf, dev(cc=other))
    rows = metric.shape[0]
    flip[0] = abuf[:, :, mine_cols].reshape(rows, half).T
    half_copy.wait_recv()
    flip[1] = pbuf[...].reshape(rows, half).T
    metric_copy.wait_recv()

    def lanes(q):
        return pl.ds(q * step, step)

    second, first = [], []
    for q in range(CHUNKS):
        pf[:, lanes(q)] = (jnp.dot(flip[0], metric[:, lanes(q)], preferred_element_type=F32)
                           + jnp.dot(flip[1], mpart[:, lanes(q)], preferred_element_type=F32))
        far = (y + 2) % 4 * 64
        made = []
        for side, to in ((0, yl), (1, yr)):
            code, scale = encode(pf[pl.ds(pl.multiple_of(far + side * 32, 32), 32), lanes(q)])
            e2[side, :, lanes(q)] = code
            s2[q, side] = scale
            made.append((copy(e2.at[side, :, lanes(q)], r2.at[side, :, lanes(q)], dev(yy=to)),
                         copy(s2.at[q, side], t2.at[q, side], dev(yy=to))))
        second.append(made)

    def pass_on(q):
        made = []
        for side, to in ((0, yl), (1, yr)):
            for item in second[q][side]:
                item.wait_recv()
            block = pf[pl.ds(pl.multiple_of(to * 64, 64), 64), lanes(q)]
            got = decode(r2[side, :, lanes(q)], t2[q, side])
            zero = jnp.zeros_like(got)
            block = block + jnp.concatenate([got, zero] if side == 0 else [zero, got], axis=0)
            code, scale = encode(block)
            e1[side, :, lanes(q)] = code
            s1[q, side] = scale
            made.append((copy(e1.at[side, :, lanes(q)], r1.at[side, :, lanes(q)], dev(yy=to)),
                         copy(s1.at[q, side], t1.at[q, side], dev(yy=to))))
        first.append(made)

    flight = {}

    def begin(q):
        for side in range(2):
            for item in first[q][side]:
                item.wait_recv()
        total = pf[pl.ds(pl.multiple_of(y * 64, 64), 64), lanes(q)]
        for side in range(2):
            total = total + decode(r1[side, :, lanes(q)], t1[q, side])
        fitted = total.astype(BF16)
        kv[z, x, c, :, lanes(q)] = fitted
        qb[y, :, lanes(q)] = fitted
        top, low = pl.ds(0, 32), pl.ds(32, 32)
        mine_top = kv.at[z, x, c, top, lanes(q)]
        mine_low = kv.at[z, x, c, low, lanes(q)]
        mine_q = qb.at[y, :, lanes(q)]
        flight["x1", q] = (copy(mine_top, mine_top, dev(xx=xl)), copy(mine_top, mine_top, dev(xx=xr)))
        flight["z1", q] = (copy(mine_low, mine_low, dev(zz=zl)), copy(mine_low, mine_low, dev(zz=zr)))
        flight["q1", q] = (copy(mine_q, mine_q, dev(yy=yl)), copy(mine_q, mine_q, dev(yy=yr)))

    def relay(q):
        toward_left, toward_right = flight["x1", q]
        toward_right.wait_recv()
        piece = kv.at[z, xl, c, pl.ds(0, 16), lanes(q)]
        right = copy(piece, piece, dev(xx=xr))
        toward_left.wait_recv()
        piece = kv.at[z, xr, c, pl.ds(16, 16), lanes(q)]
        flight["x2", q] = (copy(piece, piece, dev(xx=xl)), right)
        toward_left, toward_right = flight["z1", q]
        toward_right.wait_recv()
        piece = kv.at[zl, x, c, pl.ds(32, 16), lanes(q)]
        right = copy(piece, piece, dev(zz=zr))
        toward_left.wait_recv()
        piece = kv.at[zr, x, c, pl.ds(48, 16), lanes(q)]
        flight["z2", q] = (copy(piece, piece, dev(zz=zl)), right)
        toward_left, toward_right = flight["q1", q]
        toward_right.wait_recv()
        piece = qb.at[yl, pl.ds(0, 32), lanes(q)]
        right = copy(piece, piece, dev(yy=yr))
        toward_left.wait_recv()
        piece = qb.at[yr, pl.ds(32, 32), lanes(q)]
        flight["q2", q] = (copy(piece, piece, dev(yy=yl)), right)

    def widen(q):
        for made in flight["x2", q]:
            made.wait_recv()
        line = kv.at[z, :, c, pl.ds(0, 32), lanes(q)]
        flight["z3", q] = (copy(line, line, dev(zz=zl)), copy(line, line, dev(zz=zr)))
        for made in flight["z2", q]:
            made.wait_recv()
        line = kv.at[:, x, c, pl.ds(32, 32), lanes(q)]
        flight["x3", q] = (copy(line, line, dev(xx=xl)), copy(line, line, dev(xx=xr)))

    def relay_lines(q):
        toward_left, toward_right = flight["z3", q]
        toward_right.wait_recv()
        line = kv.at[zl, pl.ds(0, 2), c, pl.ds(0, 32), lanes(q)]
        right = copy(line, line, dev(zz=zr))
        toward_left.wait_recv()
        line = kv.at[zr, pl.ds(2, 2), c, pl.ds(0, 32), lanes(q)]
        flight["z4", q] = (copy(line, line, dev(zz=zl)), right)
        toward_left, toward_right = flight["x3", q]
        toward_right.wait_recv()
        line = kv.at[pl.ds(0, 2), xl, c, pl.ds(32, 32), lanes(q)]
        right = copy(line, line, dev(xx=xr))
        toward_left.wait_recv()
        line = kv.at[pl.ds(2, 2), xr, c, pl.ds(32, 32), lanes(q)]
        flight["x4", q] = (copy(line, line, dev(xx=xl)), right)

    def share(q):
        for made in flight["z4", q] + flight["x4", q]:
            made.wait_recv()
        plane = kv.at[:, :, c, :, lanes(q)]
        flight["core", q] = copy(plane, plane, dev(cc=other))

    def score(q):
        for made in flight["q2", q]:
            made.wait_recv()
        flight["core", q].wait_recv()
        queries = qb[:, :, lanes(q)].reshape(half, step)

        @pl.loop(0, 8)
        def _(j):
            keys = kv[j // 2, pl.ds(j % 2 * 2, 2), :, :, lanes(q)].reshape(half, step)
            part = flipped_dot(queries, keys)
            if q == 0:
                scores[j] = part
            else:
                scores[j] = scores[j] + part

    pass_on(0)
    begin(0)
    relay(0)
    widen(0)
    for q in range(CHUNKS):
        more = q + 1 < CHUNKS
        if more:
            pass_on(q + 1)
            begin(q + 1)
        relay_lines(q)
        if more:
            relay(q + 1)
            widen(q + 1)
        share(q)
        if q > 0:
            score(q - 1)
    score(CHUNKS - 1)

    for made in weights:
        made.wait_recv()
    wsum[...] = jnp.sum(wbuf[...], axis=0)
    mine_occ = p // 2
    wrow = wsum[pl.ds(mine_occ, 1), :]

    from_virt = virt[:, pl.ds(pl.multiple_of(x % 2 * 512 + c * half, half), half)] - occ[mine_occ]
    query_e = jnp.broadcast_to(from_virt, (8, half)).T[:, 0:1]
    for j in range(8):
        key_e = near[...] - occ[j]
        amp[j] = (scores[j] / (query_e + key_e)).astype(BF16)

    piece = naux // 8

    def gradient(at, slot):
        where = pl.ds(pl.multiple_of(at * piece, 128), piece)
        total = None
        for j in range(8):
            keys = kv[j // 2, pl.ds(j % 2 * 2, 2), :, :, where].reshape(half, piece)
            part = wrow[:, j:j + 1] * jnp.dot(amp[j], keys, preferred_element_type=F32)
            total = part if total is None else total + part
        gt[slot] = total

    far_made = []
    for cc in range(2):
        gradient((y + 2) % 4 * 2 + cc, cc)
        made = []
        for side, to in ((0, yl), (1, yr)):
            gs2[side, cc] = gt[cc, pl.ds(side * 128, 128), :].astype(BF16)
            made.append(copy(gs2.at[side, cc], gr2.at[side, cc], dev(yy=to)))
        far_made.append(made)
    base = counter[0]
    near_made = []
    for cc in range(2):
        for side, to in ((0, yl), (1, yr)):
            gradient(to * 2 + cc, side)
        for side, to in ((0, yl), (1, yr)):
            far_made[cc][side].wait_recv()
            add = pl.ds(side * 128, 128)
            gt[side, add, :] = gt[side, add, :] + gr2[side, cc].astype(F32)
            gs1[side, cc] = gt[side].astype(BF16)
            near_made.append(copy(gs1.at[side, cc], gr1.at[side, c], dev(yy=to, cc=cc), recv_at=base + side * 2 + c))
    gradient(y * 2 + other, 0)
    gp[...] = gt[0].astype(BF16)
    core_made = copy(gp, gpr, dev(cc=other))
    gradient(y * 2 + c, 1)

    for side in range(2):
        for core in range(2):
            pltpu.make_async_remote_copy(
                src_ref=gs1.at[side, core], dst_ref=gr1.at[side, core], send_sem=send.at[base],
                recv_sem=recv.at[base + side * 2 + core], device_id=dev(cc=other), device_id_type=MESH).wait_recv()
    core_made.wait_recv()
    mine = gt[1] + gr1[0, c].astype(F32) + gr1[1, c].astype(F32)
    out[:, mine_cols] = mine.T
    theirs = gpr[...].astype(F32) + gr1[0, other].astype(F32) + gr1[1, other].astype(F32)
    out[:, other_cols] = theirs.T
    for made in started:
        made.wait_send()
    assert counter[0] <= send.shape[0]


COPIES = 192


def on_device(integrals, metric, occ_energy, virt_energy, pair_table, pair_count):
    naux = metric.shape[1]
    y = lax.axis_index("aux") // 2
    near = lax.dynamic_index_in_dim(virt_energy.reshape(4, 4, 64), y, 1, keepdims=False).reshape(1, 256)
    vm = pl.BlockSpec(memory_space=pltpu.VMEM)
    sm = pl.BlockSpec(memory_space=pltpu.SMEM)
    V = pltpu.VMEM
    return pl.pallas_call(
        kernel,
        out_shape=jax.ShapeDtypeStruct((384, 512), F32),
        in_specs=[vm, vm, vm, vm, sm, sm, sm],
        out_specs=vm,
        scratch_shapes=[
            V((4, 4, 2, 64, naux), BF16),
            V((4, 64, naux), BF16),
            V((16, 24, 512), BF16),
            V((16, 24, 256), BF16),
            V((384, naux), BF16),
            V((2, 256, 384), BF16),
            V((16, 8, 128), F32),
            V((8, 128), F32),
            V((256, naux), F32),
            V((2, 32, naux), I16), V((CHUNKS, 2, 8, 128), F32), V((2, 32, naux), I16), V((CHUNKS, 2, 8, 128), F32),
            V((2, 64, naux), I16), V((CHUNKS, 2, 8, 128), F32), V((2, 64, naux), I16), V((CHUNKS, 2, 8, 128), F32),
            V((8, 256, 256), F32),
            V((8, 256, 256), BF16),
            V((2, 256, 384), F32),
            V((2, 2, 128, 384), BF16), V((2, 2, 128, 384), BF16),
            V((2, 2, 256, 384), BF16), V((2, 2, 256, 384), BF16),
            V((256, 384), BF16), V((256, 384), BF16),
            pltpu.SemaphoreType.DMA((COPIES,)),
            pltpu.SemaphoreType.DMA((COPIES,)),
        ],
        compiler_params=pltpu.CompilerParams(
            collective_id=0, has_side_effects=True, vmem_limit_bytes=60 * 1024 * 1024),
    )(integrals, metric, virt_energy.reshape(1, -1), near, occ_energy, pair_table, pair_count)


def solution(mesh):
    placed = (P(("aux", "pair"), None), P("aux", None), P(), P(), P("pair", None), P("pair"))
    return jax.shard_map(
        on_device, mesh=mesh, in_specs=placed, out_specs=P("aux", "pair"), check_vma=False
    )
```

time: 271 us -> 118 us (0.44)
  waiting for transfers between devices: 120 us -> 0 us
  Pallas kernels: 0 us -> 114 us
  matrix products: 60.7 us -> 0 us
  blocking collectives: 51.2 us -> 0 us
  between operations: 14 us -> 0.66 us
  other arithmetic: 12.4 us -> 0 us
  local copies, waits for them, and re-layouts: 11.9 us -> 3.5 us
    pallas_call x0 -> x1, Pallas kernels: none -> 114 us  [on_device(): pl.pallas_call(kernel, out_shape=jax.ShapeDtypeStruct((384, 512), F32), i...]
    reduce_scatter x2 -> x0, waiting for transfers between devices: 82.6 us -> none  [the longest x1 41.8 us: on_device(): out = lax.psum_scatter(grad, 'aux', scatter_dimension=1, tiled=True)]
    dot_general x11 -> x0, matrix products: 60.7 us -> none  [the longest x8 48.6 us: on_device(): jnp.dot(amplitude[:, j * per:(j + 1) * per], keys[j * per:(j + 1) * per],...]
    all_gather x2 -> x0, waiting for transfers between devices: 37 us -> none  [the longest x1 36.9 us: on_device(): keys = lax.all_gather(shard, 'pair', axis=0, tiled=True)]
    psum x1 -> x0, blocking collectives: 33.7 us -> none  [on_device(): weight = lax.psum(mine + mine.T, 'pair')]
    all_to_all x1 -> x0, blocking collectives: 17.4 us -> none  [on_device(): lax.all_to_all(integrals, 'pair', split_axis=1, concat_axis=0, tiled=True)]
    gather x8 -> x0, other arithmetic: 10.3 us -> none  [the longest x3 5.16 us: on_device(): o_query = occ_energy[query_col // virt]]
    gather x3 -> x0, local copies, waits for them, and re-layouts: 7.5 us -> none  [the longest x1 4.53 us: on_device(): e_key = virt_energy[key_col % virt]]
  transfers between devices with their start and end apart: 4 -> 0, of which waited for: 3 -> 0; matrix products, arithmetic and copies ran while one was open for 7% -> 0% of each run, Pallas kernels for 0% -> 0%
where the time goes in v2:
time: 118 us
  Pallas kernels  114 us (97%)
  local copies, waits for them, and re-layouts  3.5 us (3%)
    pallas_call x1, Pallas kernels, on_device(): pl.pallas_call(kernel, out_shape=jax.ShapeDtypeStruct((384, 512), F32), i...  114 us

profile of v2, /device:TPU:1, one launch (start us, length us, event | category | flops | bytes accessed | tf_op | source)
XLA Modules:
  0.0 117.9 jit_solution(15543837021950325820)
XLA Ops:
  0.7 0.8 reshape.11
  1.4 0.6 reshape.12.near
  2.1 113.7 %shard_map.64 = f32[384,512]{1,0:T(8,128)} custom-call(bf16[24,8192]{1,0:T(8,128)(2,1)} %ints.1, bf16[384,3072]{1,0:T(8,128)(2,1)} %metric.1, f32[1,1024]{1,0:T(1,128)} %bitcast.1, f32[1,256]{1,0:T(1,128)} %reshape.12.near, f32[8]{0:T(128)} %occ.1, s32[2,2]{1,0:T(2,128)} %tab.1, s32[1]{0:T(128)S(6)} %copy.8.cnt), custom_call_target="tpu_custom_call" | custom-call | tf_op jit(solution)/shard_map/pallas_call | solution.py:316
  115.8 2.1 %copy.9 = f32[384,512]{1,0:T(8,128)} copy(f32[384,512]{1,0:T(8,128)} %shard_map.64) | data formatting | bytes 1572864
  (1 shorter events, 0.0 us)

commit v3 on v2

--- a/solution.py
+++ b/solution.py
@@ -203,15 +203,28 @@
         flight["x4", q] = (copy(line, line, dev(xx=xl)), right)
 
     def share(q):
+        made = []
+        for zz in (z, zl, zr):
+            line = kv.at[zz, :, c, pl.ds(0, 32), lanes(q)]
+            made.append(copy(line, line, dev(cc=other)))
+        for xx in (x, xl, xr):
+            line = kv.at[:, xx, c, pl.ds(32, 32), lanes(q)]
+            made.append(copy(line, line, dev(cc=other)))
+        flight["core", q] = made
+
+    def share_far(q):
         for made in flight["z4", q] + flight["x4", q]:
             made.wait_recv()
-        plane = kv.at[:, :, c, :, lanes(q)]
-        flight["core", q] = copy(plane, plane, dev(cc=other))
+        line = kv.at[(z + 2) % 4, :, c, pl.ds(0, 32), lanes(q)]
+        flight["core", q].append(copy(line, line, dev(cc=other)))
+        line = kv.at[:, (x + 2) % 4, c, pl.ds(32, 32), lanes(q)]
+        flight["core", q].append(copy(line, line, dev(cc=other)))
 
     def score(q):
         for made in flight["q2", q]:
             made.wait_recv()
-        flight["core", q].wait_recv()
+        for made in flight["core", q]:
+            made.wait_recv()
         queries = qb[:, :, lanes(q)].reshape(half, step)
 
         @pl.loop(0, 8)
@@ -223,23 +236,10 @@
             else:
                 scores[j] = scores[j] + part
 
-    pass_on(0)
-    begin(0)
-    relay(0)
-    widen(0)
-    for q in range(CHUNKS):
-        more = q + 1 < CHUNKS
-        if more:
-            pass_on(q + 1)
-            begin(q + 1)
-        relay_lines(q)
-        if more:
-            relay(q + 1)
-            widen(q + 1)
-        share(q)
-        if q > 0:
-            score(q - 1)
-    score(CHUNKS - 1)
+    stages = ((pass_on, -1.5), (begin, 1.2), (relay, 2.3), (widen, 3.4), (relay_lines, 5.5), (share, 5.55), (share_far, 7.6), (score, 9.7))
+    order = [(at + 2 * q, q, run) for run, at in stages for q in range(CHUNKS)]
+    for _, q, run in sorted(order, key=lambda item: item[:2]):
+        run(q)
 
     for made in weights:
         made.wait_recv()
@@ -303,7 +303,7 @@
     assert counter[0] <= send.shape[0]
 
 
-COPIES = 192
+COPIES = 256
 
 
 def on_device(integrals, metric, occ_energy, virt_energy, pair_table, pair_count):

time: 118 us -> 103 us (0.87)
  Pallas kernels: 114 us -> 98.4 us
    pallas_call x1, Pallas kernels: 114 us -> 98.4 us  [on_device(): pl.pallas_call(kernel, out_shape=jax.ShapeDtypeStruct((384, 512), F32), i...]
where the time goes in v3:
time: 103 us
  Pallas kernels  98.4 us (96%)
  local copies, waits for them, and re-layouts  3.5 us (3%)
    pallas_call x1, Pallas kernels, on_device(): pl.pallas_call(kernel, out_shape=jax.ShapeDtypeStruct((384, 512), F32), i...  98.4 us
    unnamed x1, local copies, waits for them, and re-layouts  2.06 us

profile of v3, /device:TPU:1, one launch (start us, length us, event | category | flops | bytes accessed | tf_op | source)
XLA Modules:
  0.0 102.6 jit_solution(13378845954894584428)
XLA Ops:
  0.7 0.8 reshape.11
  1.4 0.6 reshape.12.near
  2.1 98.4 %shard_map.64 = f32[384,512]{1,0:T(8,128)} custom-call(bf16[24,8192]{1,0:T(8,128)(2,1)} %ints.1, bf16[384,3072]{1,0:T(8,128)(2,1)} %metric.1, f32[1,1024]{1,0:T(1,128)} %bitcast.1, f32[1,256]{1,0:T(1,128)} %reshape.12.near, f32[8]{0:T(128)} %occ.1, s32[2,2]{1,0:T(2,128)} %tab.1, s32[1]{0:T(128)S(6)} %copy.8.cnt), custom_call_target="tpu_custom_call" | custom-call | tf_op jit(solution)/shard_map/pallas_call | solution.py:316
  100.5 2.1 %copy.9 = f32[384,512]{1,0:T(8,128)} copy(f32[384,512]{1,0:T(8,128)} %shard_map.64) | data formatting | bytes 1572864
  (1 shorter events, 0.0 us)

commit v4 on v3

--- a/solution.py
+++ b/solution.py
@@ -9,12 +9,12 @@
 
 MESH = pl.DeviceIdType.MESH
 F32, BF16, I16 = jnp.float32, jnp.bfloat16, jnp.int16
-CHUNKS = 4
+CHUNKS = 3
+FIT, PASS = (-8, 1), (-5.5, 1)
+BEGIN, RELAY, WIDEN = (1.2, 0.9), (2.2, 0.9), (3.3, 2)
+ASK, REASK = (1.25, 0.9), (5.2, 2)
+LINES, SHARE, FAR, SCORE = (5.5, 2), (5.55, 2), (7.6, 2), (9.7, 2)
 LEVELS = 32000.0
-
-
-def flipped_dot(a, b):
-    return lax.dot_general(a, b, (((1,), (1,)), ((), ())), preferred_element_type=F32)
 
 
 def encode(x):
@@ -27,10 +27,10 @@
 
 
 def kernel(ints, metric, virt, near, occ, tab, cnt, out,
-           kv, qb, abuf, pbuf, mpart, flip, wbuf, wsum, pf,
+           kv, qb, abuf, pbuf, mfull, flip, wbuf, wsum, pf,
            e2, s2, r2, t2, e1, s1, r1, t1,
-           scores, amp, gt, gs2, gr2, gs1, gr1, gp, gpr,
-           send, recv):
+           turned, scores, amp, gt, gs2, gr2, gs1, gr1, gp, gpr,
+           send, recv, local):
     p = lax.axis_index("pair")
     alpha = lax.axis_index("aux")
     z, x = p // 4, p % 4
@@ -76,6 +76,8 @@
         hits = jnp.where((row == i) & (lane == j), 1.0, 0.0) + jnp.where((row == j) & (lane == i), 1.0, 0.0)
         counts = counts + live * hits
     wbuf[p] = counts
+    own_metric = pltpu.make_async_copy(metric, mfull.at[0], local)
+    own_metric.start()
     pl.semaphore_wait(barrier, len(peers))
 
     gathers = []
@@ -83,7 +85,7 @@
         to = (p + d) % n_pair
         where = {"pair": to, "aux": alpha}
         gathers.append(copy(ints.at[:, pl.ds(pl.multiple_of(to * 512, 512), 512)], abuf.at[p], where))
-    metric_copy = copy(metric, mpart, dev(cc=other))
+    metric_copy = copy(metric, mfull.at[1], dev(cc=other))
     weights = []
     for d in range(1, n_pair):
         where = {"pair": (p + d) % n_pair, "aux": alpha}
@@ -95,18 +97,20 @@
     other_cols = pl.ds(pl.multiple_of(other * half, half), half)
     half_copy = copy(abuf.at[:, :, other_cols], pbuf, dev(cc=other))
     rows = metric.shape[0]
-    flip[0] = abuf[:, :, mine_cols].reshape(rows, half).T
+    flip[:, 0:rows] = abuf[:, :, mine_cols].reshape(rows, half).T
     half_copy.wait_recv()
-    flip[1] = pbuf[...].reshape(rows, half).T
+    flip[:, rows:2 * rows] = pbuf[...].reshape(rows, half).T
+    own_metric.wait()
     metric_copy.wait_recv()
 
     def lanes(q):
         return pl.ds(q * step, step)
 
-    second, first = [], []
-    for q in range(CHUNKS):
-        pf[:, lanes(q)] = (jnp.dot(flip[0], metric[:, lanes(q)], preferred_element_type=F32)
-                           + jnp.dot(flip[1], mpart[:, lanes(q)], preferred_element_type=F32))
+    second, first = [None] * CHUNKS, [None] * CHUNKS
+
+    def fit(q):
+        pf[:, lanes(q)] = jnp.dot(
+            flip[...], mfull[:, :, lanes(q)].reshape(2 * rows, step), preferred_element_type=F32)
         far = (y + 2) % 4 * 64
         made = []
         for side, to in ((0, yl), (1, yr)):
@@ -115,7 +119,7 @@
             s2[q, side] = scale
             made.append((copy(e2.at[side, :, lanes(q)], r2.at[side, :, lanes(q)], dev(yy=to)),
                          copy(s2.at[q, side], t2.at[q, side], dev(yy=to))))
-        second.append(made)
+        second[q] = made
 
     def pass_on(q):
         made = []
@@ -131,7 +135,7 @@
             s1[q, side] = scale
             made.append((copy(e1.at[side, :, lanes(q)], r1.at[side, :, lanes(q)], dev(yy=to)),
                          copy(s1.at[q, side], t1.at[q, side], dev(yy=to))))
-        first.append(made)
+        first[q] = made
 
     flight = {}
 
@@ -148,10 +152,8 @@
         top, low = pl.ds(0, 32), pl.ds(32, 32)
         mine_top = kv.at[z, x, c, top, lanes(q)]
         mine_low = kv.at[z, x, c, low, lanes(q)]
-        mine_q = qb.at[y, :, lanes(q)]
         flight["x1", q] = (copy(mine_top, mine_top, dev(xx=xl)), copy(mine_top, mine_top, dev(xx=xr)))
         flight["z1", q] = (copy(mine_low, mine_low, dev(zz=zl)), copy(mine_low, mine_low, dev(zz=zr)))
-        flight["q1", q] = (copy(mine_q, mine_q, dev(yy=yl)), copy(mine_q, mine_q, dev(yy=yr)))
 
     def relay(q):
         toward_left, toward_right = flight["x1", q]
@@ -168,6 +170,12 @@
         toward_left.wait_recv()
         piece = kv.at[zr, x, c, pl.ds(48, 16), lanes(q)]
         flight["z2", q] = (copy(piece, piece, dev(zz=zl)), right)
+
+    def ask(q):
+        mine_q = qb.at[y, :, lanes(q)]
+        flight["q1", q] = (copy(mine_q, mine_q, dev(yy=yl)), copy(mine_q, mine_q, dev(yy=yr)))
+
+    def relay_ask(q):
         toward_left, toward_right = flight["q1", q]
         toward_right.wait_recv()
         piece = qb.at[yl, pl.ds(0, 32), lanes(q)]
@@ -225,19 +233,20 @@
             made.wait_recv()
         for made in flight["core", q]:
             made.wait_recv()
-        queries = qb[:, :, lanes(q)].reshape(half, step)
+        turned[...] = qb[:, :, lanes(q)].reshape(half, step).T
 
         @pl.loop(0, 8)
         def _(j):
             keys = kv[j // 2, pl.ds(j % 2 * 2, 2), :, :, lanes(q)].reshape(half, step)
-            part = flipped_dot(queries, keys)
+            part = jnp.dot(keys, turned[...], preferred_element_type=F32)
             if q == 0:
                 scores[j] = part
             else:
                 scores[j] = scores[j] + part
 
-    stages = ((pass_on, -1.5), (begin, 1.2), (relay, 2.3), (widen, 3.4), (relay_lines, 5.5), (share, 5.55), (share_far, 7.6), (score, 9.7))
-    order = [(at + 2 * q, q, run) for run, at in stages for q in range(CHUNKS)]
+    stages = ((fit, FIT), (pass_on, PASS), (begin, BEGIN), (relay, RELAY), (ask, ASK), (relay_ask, REASK), (widen, WIDEN),
+              (relay_lines, LINES), (share, SHARE), (share_far, FAR), (score, SCORE))
+    order = [(at[0] + at[1] * q, q, run) for run, at in stages for q in range(CHUNKS)]
     for _, q, run in sorted(order, key=lambda item: item[:2]):
         run(q)
 
@@ -248,10 +257,9 @@
     wrow = wsum[pl.ds(mine_occ, 1), :]
 
     from_virt = virt[:, pl.ds(pl.multiple_of(x % 2 * 512 + c * half, half), half)] - occ[mine_occ]
-    query_e = jnp.broadcast_to(from_virt, (8, half)).T[:, 0:1]
+    key_e = jnp.broadcast_to(near[...], (8, half)).T[:, 0:1]
     for j in range(8):
-        key_e = near[...] - occ[j]
-        amp[j] = (scores[j] / (query_e + key_e)).astype(BF16)
+        amp[j] = (scores[j] / (key_e + (from_virt - occ[j]))).T.astype(BF16)
 
     piece = naux // 8
 
@@ -316,20 +324,21 @@
     return pl.pallas_call(
         kernel,
         out_shape=jax.ShapeDtypeStruct((384, 512), F32),
-        in_specs=[vm, vm, vm, vm, sm, sm, sm],
+        in_specs=[vm, pl.BlockSpec(memory_space=pl.ANY), vm, vm, sm, sm, sm],
         out_specs=vm,
         scratch_shapes=[
             V((4, 4, 2, 64, naux), BF16),
             V((4, 64, naux), BF16),
             V((16, 24, 512), BF16),
             V((16, 24, 256), BF16),
-            V((384, naux), BF16),
-            V((2, 256, 384), BF16),
+            V((2, 384, naux), BF16),
+            V((256, 768), BF16),
             V((16, 8, 128), F32),
             V((8, 128), F32),
             V((256, naux), F32),
             V((2, 32, naux), I16), V((CHUNKS, 2, 8, 128), F32), V((2, 32, naux), I16), V((CHUNKS, 2, 8, 128), F32),
             V((2, 64, naux), I16), V((CHUNKS, 2, 8, 128), F32), V((2, 64, naux), I16), V((CHUNKS, 2, 8, 128), F32),
+            V((naux // CHUNKS, 256), BF16),
             V((8, 256, 256), F32),
             V((8, 256, 256), BF16),
             V((2, 256, 384), F32),
@@ -338,6 +347,7 @@
             V((256, 384), BF16), V((256, 384), BF16),
             pltpu.SemaphoreType.DMA((COPIES,)),
             pltpu.SemaphoreType.DMA((COPIES,)),
+            pltpu.SemaphoreType.DMA(()),
         ],
         compiler_params=pltpu.CompilerParams(
             collective_id=0, has_side_effects=True, vmem_limit_bytes=60 * 1024 * 1024),

time: 103 us -> 98 us (0.951)
  Pallas kernels: 98.4 us -> 93.7 us
    pallas_call x1, Pallas kernels: 98.4 us -> 93.7 us  [on_device(): pl.pallas_call(kernel, out_shape=jax.ShapeDtypeStruct((384, 512), F32), i...]
where the time goes in v4:
time: 98 us; the launch traced here: 97.8 us
  Pallas kernels  93.7 us (96%)
  local copies, waits for them, and re-layouts  3.5 us (4%)
    pallas_call x1, Pallas kernels, on_device(): pl.pallas_call(kernel, out_shape=jax.ShapeDtypeStruct((384, 512), F32), i...  93.7 us
    unnamed x1, local copies, waits for them, and re-layouts  2.06 us

profile of v4, /device:TPU:1, one launch (start us, length us, event | category | flops | bytes accessed | tf_op | source)
XLA Modules:
  0.0 97.8 jit_solution(7513023682690282302)
XLA Ops:
  0.7 0.8 reshape.11
  1.4 0.6 reshape.12.near
  2.1 93.7 %shard_map.64 = f32[384,512]{1,0:T(8,128)} custom-call(bf16[24,8192]{1,0:T(8,128)(2,1)} %ints.1, bf16[384,3072]{1,0:T(8,128)(2,1)} %metric.1, f32[1,1024]{1,0:T(1,128)} %bitcast.1, f32[1,256]{1,0:T(1,128)} %reshape.12.near, f32[8]{0:T(128)} %occ.1, s32[2,2]{1,0:T(2,128)} %tab.1, s32[1]{0:T(128)S(6)} %copy.8.cnt), custom_call_target="tpu_custom_call" | custom-call | tf_op jit(solution)/shard_map/pallas_call | solution.py:324
  95.8 2.1 %copy.9 = f32[384,512]{1,0:T(8,128)} copy(f32[384,512]{1,0:T(8,128)} %shard_map.64) | data formatting | bytes 1572864
  (1 shorter events, 0.0 us)
